TPU v7x, 512 devices: a whole 4x8x8 slice. The times are simulated.
512 devices in a mesh: ep: 16 (over z_hi, y), sp: 32 (over z_lo, x, core).
Axes of the slice: x: 4, y: 8, z: 8 (z_hi: 2, z_lo: 4; z = z_hi * 4 + z_lo), core: 2. Of those that a mesh axis runs over, the one named last changes fastest.
Arguments:
- grad_out: bfloat16 [65536, 4096], P(('ep', 'sp')), may hold values from -1.5 to 1.5
- routes: int32 [65536, 8], P(('ep', 'sp')), may hold values from 0 to 127, as said below
- gate: bfloat16 [65536, 8], P(('ep', 'sp')), may hold values from 0.049804688 to 1
- saved: bfloat16 [16, 32, 256, 3072], P('ep', 'sp'), may hold values from -6 to 6
- w_down: bfloat16 [16, 1536, 4096], P('ep', None, 'sp'), may hold values from -0.15625 to 0.15625
Outputs:
- grad_pre: bfloat16 [16, 32, 256, 3072], P('ep', 'sp')
- grad_gate: float32 [65536, 8], P(('ep', 'sp'))
Inputs may be any that keep to these rules, and one draw needn't show every extreme that they name: `routes`: each row names 8 different experts. In every block of 128 rows at most 16 rows name the same expert whose number is a multiple of 8, and in every block one such expert is named by exactly 16 rows; it is the same expert for all blocks whose indices agree modulo 32.
All inputs are finite; a program needn't handle non-finite values.
Results may differ from a plain program's by a relative error of at most 0.0029.
Values may be sent and summed in bfloat16 or wider, within the bound.
No kernel may reach another device: no remote copies, remote signals or barrier semaphores. Data moves between devices by JAX's collectives and lax.ppermute only.
A program may use at most 128 MiB of HBM per device.

v0:
```python
import math
import jax
import jax.numpy as jnp
from jax import lax
from jax.sharding import PartitionSpec as P

EXPERTS = 128


def side_by_side(arrays, axis, split_dim, concat_dim, along):
    widths = [math.prod(a.shape[along:]) for a in arrays]
    both = jnp.concatenate(
        [a.reshape(*a.shape[:along], w) for a, w in zip(arrays, widths)], axis=along
    )
    whole = lax.all_to_all(both, axis, split_axis=split_dim, concat_axis=concat_dim, tiled=True)
    tiles = jnp.split(whole, [sum(widths[:k]) for k in range(1, len(widths))], axis=along)
    return tuple((b.reshape(*whole.shape[:along], *a.shape[along:]) for a, b in zip(arrays, tiles)))


def on_device(grad_out, routes, gate, saved, w_down):
    ep_count = lax.axis_size("ep")
    experts_each = EXPERTS // ep_count
    model_width = grad_out.shape[1]
    slot_count = saved.shape[2]
    capacity = slot_count // ep_count
    hidden_units = saved.shape[3] // 2
    flight = routes % experts_each == 0
    owners = routes // experts_each
    wave_ids = jnp.arange(ep_count, dtype=jnp.int32)
    onehot = (owners[:, :, None] == wave_ids[None, None, :]) & flight[:, :, None]
    member = jnp.sum(onehot.astype(jnp.int32), axis=1)
    gate_by_expert = jnp.sum(
        onehot.astype(jnp.float32) * gate.astype(jnp.float32)[:, :, None], axis=1
    )
    places = jnp.cumsum(member, axis=0) - member
    place_ids = jnp.arange(capacity, dtype=jnp.int32)
    chosen = (places.T[:, None, :] == place_ids[None, :, None]) & (member.T[:, None, :] > 0)
    chosen_float = chosen.astype(jnp.float32)
    outgoing = jnp.einsum(
        "fct,td->fcd", chosen.astype(jnp.bfloat16), grad_out, preferred_element_type=jnp.float32
    ).astype(jnp.bfloat16)
    gate_out = jnp.einsum(
        "fct,tf->fc", chosen_float, gate_by_expert, precision=lax.Precision.HIGHEST
    ).astype(jnp.bfloat16)
    gate_pre = saved[0, 0, :, :hidden_units].astype(jnp.float32)
    up_pre = saved[0, 0, :, hidden_units:].astype(jnp.float32)
    sigmoid_gate = jax.nn.sigmoid(gate_pre)
    silu_gate = gate_pre * sigmoid_gate
    hidden = (silu_gate * up_pre).astype(jnp.bfloat16)
    arrived, gate_in = side_by_side((outgoing, gate_out), "ep", 0, 0, 2)
    arrived = arrived.reshape(slot_count, model_width)
    gate_in = gate_in.reshape(slot_count).astype(jnp.float32)
    grad_hidden = lax.dot_general(
        arrived,
        lax.all_gather(w_down, "sp", axis=2, tiled=True)[0],
        (((1,), (1,)), ((), ())),
        preferred_element_type=jnp.float32,
    )
    score_values = jnp.sum(
        grad_hidden * lax.optimization_barrier(hidden).astype(jnp.float32), axis=1
    )
    scaled = grad_hidden * gate_in[:, None]
    grad_gate_pre = scaled * up_pre * sigmoid_gate * (1.0 + gate_pre * (1.0 - sigmoid_gate))
    grad_up_pre = scaled * silu_gate
    grad_pre = (
        jnp.concatenate([grad_gate_pre, grad_up_pre], axis=1)
        .astype(jnp.bfloat16)
        .reshape(saved.shape)
    )
    returned = lax.all_to_all(
        score_values.reshape(ep_count, capacity), "ep", split_axis=0, concat_axis=0, tiled=True
    )
    score_by_expert = jnp.einsum(
        "fct,fc->tf", chosen_float, returned, precision=lax.Precision.HIGHEST
    )
    grad_gate = jnp.sum(onehot.astype(jnp.float32) * score_by_expert[:, None, :], axis=2)
    return (grad_pre, grad_gate)


def solution(mesh):
    in_specs = (
        P(("ep", "sp"), None),
        P(("ep", "sp"), None),
        P(("ep", "sp"), None),
        P("ep", "sp", None, None),
        P("ep", None, "sp"),
    )
    out_specs = (P("ep", "sp", None, None), P(("ep", "sp"), None))
    return jax.shard_map(
        on_device, mesh=mesh, in_specs=in_specs, out_specs=out_specs, check_vma=False
    )
```

profile of v0, /device:TPU:1, one launch (start us, length us, event | category | flops | bytes accessed | tf_op | source)
XLA Modules:
  0.0 214.4 jit_solution(14429993677092649671)
XLA Ops:
  7.2 0.0 copy-start
  7.2 0.0 all-gather.2.cloned.1.call-start
  7.2 0.7 all-gather.2.cloned.1.call-update
  7.9 0.7 fusion.27
  8.6 0.7 add_select_fusion.1
  9.3 0.1 copy.18
  9.4 0.2 reduce_window_sum.11
  9.6 0.1 copy.20
  9.7 0.7 convert_element_type.54
  10.4 0.2 fusion.16
  10.7 0.2 copy.21
  10.8 0.0 copy-done
  10.8 0.7 convolution_convert_fusion
  11.5 1.5 pad_maximum_fusion
  13.1 16.2 %all-to-all-start = ((bf16[16,16,4097]{2,1,0:T(8,128)(2,1)}), bf16[16,16,4097]{2,1,0:T(8,128)(2,1)S(1)}, u32[]{:S(2)}, u32[]{:S(2)}) async-start(bf16[16,16,4097]{2,1,0:T(8,128)(2,1)} %pad_maximum_fusion), calls=%async_computation | async-start | bytes 4325376 | tf_op jit(solution)/shard_map/all_to_all | solution.py:15
  29.3 2.9 %fusion.5 = bf16[256,1536]{1,0:T(8,128)(2,1)} fusion(bf16[1,1,256,3072]{3,2,1,0:T(8,128)(2,1)} %param.8), kind=kLoop, calls=%fused_computation.12 | loop fusion | flops 3145728 | bytes 2359296 | tf_op jit(solution)/shard_map/convert_element_type | solution.py:49
  32.2 54.8 %all-to-all-done = bf16[16,16,4097]{2,1,0:T(8,128)(2,1)S(1)} async-done(((bf16[16,16,4097]{2,1,0:T(8,128)(2,1)}), bf16[16,16,4097]{2,1,0:T(8,128)(2,1)S(1)}, u32[]{:S(2)}, u32[]{:S(2)}) %all-to-all-start) | async-done | bytes 2097696 | tf_op jit(solution)/shard_map/all_to_all | solution.py:15
  86.9 0.1 convert_reduce_fusion
  87.0 0.1 reshape.66
  87.1 1.6 split.8
  88.7 81.5 %all-gather.2.cloned.1.call-done = bf16[1,1536,4096]{2,1,0:T(8,128)(2,1)} async-done(((bf16[1,1536,128]{2,1,0:T(8,128)(2,1)}), bf16[1,1536,4096]{2,1,0:T(8,128)(2,1)}) %all-gather.2.cloned.1.call-update) | async-done | bytes 12582928 | tf_op jit(solution)/shard_map/all_gather | solution.py:55
  170.2 10.0 %fusion.12 = (bf16[1,1,256,1536]{3,2,1,0:T(8,128)(2,1)S(1)}, bf16[1,1,256,1536]{3,2,1,0:T(8,128)(2,1)S(1)}, f32[256]{0:T(256)S(1)}) fusion(f32[256]{0:T(256)S(1)} %reshape.66, bf16[1,1,256,3072]{3,2,1,0:T(8,128)(2,1)} %param.8, bf16[256,1536]{1,0:T(8,128)(2,1)} %fusion.5, bf16[256,4096]{1,0:T(8,128)(2,1)} %bitcast.52, ...), kind=kOutput, calls=%fused_computation.22 | convolution fusion | flops 3228696320 | bytes 18614272 | tf_op jit(solution)/shard_map/dot_general | solution.py:53
  180.2 0.7 all_to_all.12
  180.9 14.5 %all-to-all-start.1 = ((f32[16,1,16]{2,1,0:T(1,128)}), f32[16,1,16]{2,1,0:T(1,128)S(1)}, u32[]{:S(2)}, u32[]{:S(2)}) async-start(f32[16,1,16]{2,1,0:T(1,128)} %all_to_all.12), calls=%async_computation.1 | async-start | bytes 16384 | tf_op jit(solution)/shard_map/all_to_all | solution.py:70
  195.4 1.4 pad_maximum_fusion.1
  196.8 9.9 %all-to-all-done.1 = f32[16,1,16]{2,1,0:T(1,128)S(1)} async-done(((f32[16,1,16]{2,1,0:T(1,128)}), f32[16,1,16]{2,1,0:T(1,128)S(1)}, u32[]{:S(2)}, u32[]{:S(2)}) %all-to-all-start.1) | async-done | bytes 1056 | tf_op jit(solution)/shard_map/all_to_all | solution.py:70
  206.7 0.2 fusion.14
  206.9 0.6 select_reduce_fusion
  (5 shorter events, 0.1 us)
Async XLA Ops:
  7.2 3.7 %copy-start = (bf16[128,4096]{1,0:T(8,128)(2,1)S(1)}, bf16[128,4096]{1,0:T(8,128)(2,1)}, u32[]{:S(2)}) copy-start(bf16[128,4096]{1,0:T(8,128)(2,1)} %param.5) | copy-start | bytes 3145732
  7.2 163.1 %all-gather.2.cloned.1.call-start = ((), (), s32[]{:S(2)}) async-start(), calls=%async_computation.2 | async-start | bytes 12976128 | tf_op jit(solution)/shard_map/all_gather | solution.py:55
  13.1 73.9 %all-to-all-start = ((bf16[16,16,4097]{2,1,0:T(8,128)(2,1)}), bf16[16,16,4097]{2,1,0:T(8,128)(2,1)S(1)}, u32[]{:S(2)}, u32[]{:S(2)}) async-start(bf16[16,16,4097]{2,1,0:T(8,128)(2,1)} %pad_maximum_fusion), calls=%async_computation | async-start | bytes 4325376 | tf_op jit(solution)/shard_map/all_to_all | solution.py:15
  180.9 25.8 %all-to-all-start.1 = ((f32[16,1,16]{2,1,0:T(1,128)}), f32[16,1,16]{2,1,0:T(1,128)S(1)}, u32[]{:S(2)}, u32[]{:S(2)}) async-start(f32[16,1,16]{2,1,0:T(1,128)} %all_to_all.12), calls=%async_computation.1 | async-start | bytes 16384 | tf_op jit(solution)/shard_map/all_to_all | solution.py:70
Sparse Core Ops, SparseCore 0:
  10.0 160.1 all-gather.1
where the time goes:
time: 215 us; the launch traced here: 214 us
  waiting for transfers between devices  147 us (68%)
  starting transfers between devices  30.7 us (14%)
  between operations  14.1 us (7%)
  matrix products  11.1 us (5%)
  other arithmetic  8.82 us (4%)
  local copies, waits for them, and re-layouts  2.74 us (1%)
    all_gather x1, waiting for transfers between devices, on_device(): lax.all_gather(w_down, 'sp', axis=2, tiled=True)[0]  81.5 us
    all_to_all x1, waiting for transfers between devices, side_by_side(): lax.all_to_all(both, axis, split_axis=split_dim, concat_axis=concat_dim,...  54.8 us
    all_to_all x1, starting transfers between devices, side_by_side(): lax.all_to_all(both, axis, split_axis=split_dim, concat_axis=concat_dim,...  16.2 us
    all_to_all x1, starting transfers between devices, on_device(): lax.all_to_all(score_values.reshape(ep_count, capacity), 'ep', split_axis...  14.5 us
    dot_general x1, matrix products, on_device(): lax.dot_general(arrived, lax.all_gather(w_down, 'sp', axis=2, tiled=True)...  9.98 us
    all_to_all x1, waiting for transfers between devices, on_device(): lax.all_to_all(score_values.reshape(ep_count, capacity), 'ep', split_axis...  9.89 us
  transfers between devices with their start and end apart: 3, of which 3 were waited for; matrix products, arithmetic and copies ran while one was open for 5% of the time, Pallas kernels for 0%

commit v1 on v0

--- a/solution.py
+++ b/solution.py
@@ -18,6 +18,12 @@
 
 
 def on_device(grad_out, routes, gate, saved, w_down):
+
+    def _assign_cells(row_data, ax_name):
+        reply = lax.all_to_all(jnp.stack([row_data] * lax.axis_size(ax_name)), ax_name, 0, 0)
+        w_next = jnp.concatenate(reply, axis=2)
+        return w_next
+
     ep_count = lax.axis_size("ep")
     experts_each = EXPERTS // ep_count
     model_width = grad_out.shape[1]
@@ -52,7 +58,7 @@
     gate_in = gate_in.reshape(slot_count).astype(jnp.float32)
     grad_hidden = lax.dot_general(
         arrived,
-        lax.all_gather(w_down, "sp", axis=2, tiled=True)[0],
+        _assign_cells(w_down, "sp")[0],
         (((1,), (1,)), ((), ())),
         preferred_element_type=jnp.float32,
     )

time: 215 us -> 416 us (1.93)
  waiting for transfers between devices: 147 us -> 339 us
  starting transfers between devices: 30.7 us -> 44.8 us
  between operations: 14.1 us -> 0.72 us
  local copies, waits for them, and re-layouts: 2.74 us -> 11.6 us
    all_to_all x0 -> x1, waiting for transfers between devices: none -> 274 us  [_assign_cells(): lax.all_to_all(jnp.stack([row_data] * lax.axis_size(ax_name)), ax_name, 0...]
    all_gather x1 -> x0, waiting for transfers between devices: 81.5 us -> none  [on_device(): lax.all_gather(w_down, 'sp', axis=2, tiled=True)[0]]
    all_to_all x0 -> x1, starting transfers between devices: none -> 9.08 us  [_assign_cells(): lax.all_to_all(jnp.stack([row_data] * lax.axis_size(ax_name)), ax_name, 0...]
    another operation x0 -> x2, local copies, waits for them, and re-layouts: none -> 8.8 us  [the longest x1 6.88 us: _assign_cells(): jnp.stack([row_data] * lax.axis_size(ax_name))]
    all_to_all x1, starting transfers between devices: 14.5 us -> 19.5 us  [on_device(): lax.all_to_all(score_values.reshape(ep_count, capacity), 'ep', split_axis...]
  transfers between devices with their start and end apart: 3 -> 3, of which waited for: 3 -> 3; matrix products, arithmetic and copies ran while one was open for 5% -> 2% of each run, Pallas kernels for 0% -> 0%
where the time goes in v1:
time: 416 us
  waiting for transfers between devices  339 us (81%)
  starting transfers between devices  44.8 us (11%)
  local copies, waits for them, and re-layouts  11.6 us (3%)
  matrix products  11 us (3%)
  other arithmetic  8.75 us (2%)
    all_to_all x1, waiting for transfers between devices, _assign_cells(): lax.all_to_all(jnp.stack([row_data] * lax.axis_size(ax_name)), ax_name, 0...  274 us
    all_to_all x1, waiting for transfers between devices, side_by_side(): lax.all_to_all(both, axis, split_axis=split_dim, concat_axis=concat_dim,...  54.7 us
    all_to_all x1, starting transfers between devices, on_device(): lax.all_to_all(score_values.reshape(ep_count, capacity), 'ep', split_axis...  19.5 us
    all_to_all x1, starting transfers between devices, side_by_side(): lax.all_to_all(both, axis, split_axis=split_dim, concat_axis=concat_dim,...  16.2 us
    dot_general x1, matrix products, on_device(): lax.dot_general(arrived, _assign_cells(w_down, 'sp')[0], (((1,), (1,)), (...  9.93 us
    all_to_all x1, waiting for transfers between devices, on_device(): lax.all_to_all(score_values.reshape(ep_count, capacity), 'ep', split_axis...  9.89 us
    all_to_all x1, starting transfers between devices, _assign_cells(): lax.all_to_all(jnp.stack([row_data] * lax.axis_size(ax_name)), ax_name, 0...  9.08 us
  transfers between devices with their start and end apart: 3, of which 3 were waited for; matrix products, arithmetic and copies ran while one was open for 2% of the time, Pallas kernels for 0%

profile of v1, /device:TPU:1, one launch (start us, length us, event | category | flops | bytes accessed | tf_op | source)
XLA Modules:
  0.0 416.0 jit_solution(16685171669435149848)
XLA Ops:
  0.6 0.0 copy-start
  0.6 0.8 add_select_fusion.1
  1.4 0.7 fusion.25
  2.1 0.1 copy.27
  2.3 0.2 reduce_window_sum.11
  2.4 0.1 copy.29
  2.5 0.7 convert_element_type.54
  3.2 0.2 fusion.14
  3.5 0.2 copy.30
  3.7 0.0 copy-done
  3.7 0.7 convolution_convert_fusion
  4.4 1.5 pad_maximum_fusion
  5.9 16.2 %all-to-all-start = ((bf16[16,16,4097]{2,1,0:T(8,128)(2,1)}), bf16[16,16,4097]{2,1,0:T(8,128)(2,1)S(1)}, u32[]{:S(2)}, u32[]{:S(2)}) async-start(bf16[16,16,4097]{2,1,0:T(8,128)(2,1)} %pad_maximum_fusion), calls=%async_computation | async-start | bytes 4325376 | tf_op jit(solution)/shard_map/all_to_all | solution.py:15
  22.1 1.9 copy.31
  24.0 54.7 %all-to-all-done = bf16[16,16,4097]{2,1,0:T(8,128)(2,1)S(1)} async-done(((bf16[16,16,4097]{2,1,0:T(8,128)(2,1)}), bf16[16,16,4097]{2,1,0:T(8,128)(2,1)S(1)}, u32[]{:S(2)}, u32[]{:S(2)}) %all-to-all-start) | async-done | bytes 2097696 | tf_op jit(solution)/shard_map/all_to_all | solution.py:15
  78.7 6.9 %stack.2 = bf16[32,1,1536,128]{2,3,1,0:T(8,128)(2,1)} broadcast(bf16[1536,128]{0,1:T(8,128)(2,1)} %copy.31), dimensions={2,3} | broadcast | bytes 12976128 | tf_op jit(solution)/shard_map/stack | solution.py:23
  85.6 9.1 %all-to-all-start.1 = ((bf16[32,1,1536,128]{2,3,1,0:T(8,128)(2,1)}), bf16[32,1,1536,128]{2,3,1,0:T(8,128)(2,1)}, u32[]{:S(2)}, u32[]{:S(2)}) async-start(bf16[32,1,1536,128]{2,3,1,0:T(8,128)(2,1)} %stack.2), calls=%async_computation.1 | async-start | bytes 25165824 | tf_op jit(solution)/shard_map/all_to_all | solution.py:23
  94.7 2.7 fusion.3
  97.4 0.1 convert_reduce_fusion
  97.5 0.1 reshape.73
  97.6 1.6 split.8
  99.3 274.5 %all-to-all-done.1 = bf16[32,1,1536,128]{2,3,1,0:T(8,128)(2,1)} async-done(((bf16[32,1,1536,128]{2,3,1,0:T(8,128)(2,1)}), bf16[32,1,1536,128]{2,3,1,0:T(8,128)(2,1)}, u32[]{:S(2)}, u32[]{:S(2)}) %all-to-all-start.1) | async-done | bytes 12582944 | tf_op jit(solution)/shard_map/all_to_all | solution.py:23
  373.8 9.9 %fusion.10 = (bf16[1,1,256,1536]{3,2,1,0:T(8,128)(2,1)S(1)}, bf16[1,1,256,1536]{3,2,1,0:T(8,128)(2,1)S(1)}, f32[256]{0:T(256)S(1)}) fusion(f32[256]{0:T(256)S(1)} %reshape.73, bf16[1,1,256,3072]{3,2,1,0:T(8,128)(2,1)} %param.8, bf16[256,1536]{1,0:T(8,128)(2,1)} %fusion.3, bf16[256,4096]{1,0:T(8,128)(2,1)} %bitcast.54, bf16[1536,4096]{0,1:T(8,128)(2,1)} %bitcast.12), kind=kOutput, calls=%fused_computation.20 | convolution fusion | flops 3228696320 | bytes 18614272 | tf_op jit(solution)/shard_map/dot_general | solution.py:59
  383.7 0.7 all_to_all.16
  384.4 19.5 %all-to-all-start.2 = ((f32[16,1,16]{2,1,0:T(1,128)}), f32[16,1,16]{2,1,0:T(1,128)S(1)}, u32[]{:S(2)}, u32[]{:S(2)}) async-start(f32[16,1,16]{2,1,0:T(1,128)} %all_to_all.16), calls=%async_computation.2 | async-start | bytes 16384 | tf_op jit(solution)/shard_map/all_to_all | solution.py:76
  403.9 1.4 pad_maximum_fusion.1
  405.3 9.9 %all-to-all-done.2 = f32[16,1,16]{2,1,0:T(1,128)S(1)} async-done(((f32[16,1,16]{2,1,0:T(1,128)}), f32[16,1,16]{2,1,0:T(1,128)S(1)}, u32[]{:S(2)}, u32[]{:S(2)}) %all-to-all-start.2) | async-done | bytes 1056 | tf_op jit(solution)/shard_map/all_to_all | solution.py:76
  415.2 0.2 fusion.12
  415.4 0.6 select_reduce_fusion
  (5 shorter events, 0.1 us)
Async XLA Ops:
  0.6 3.0 copy-start
  5.9 72.8 %all-to-all-start = ((bf16[16,16,4097]{2,1,0:T(8,128)(2,1)}), bf16[16,16,4097]{2,1,0:T(8,128)(2,1)S(1)}, u32[]{:S(2)}, u32[]{:S(2)}) async-start(bf16[16,16,4097]{2,1,0:T(8,128)(2,1)} %pad_maximum_fusion), calls=%async_computation | async-start | bytes 4325376 | tf_op jit(solution)/shard_map/all_to_all | solution.py:15
  85.6 288.2 %all-to-all-start.1 = ((bf16[32,1,1536,128]{2,3,1,0:T(8,128)(2,1)}), bf16[32,1,1536,128]{2,3,1,0:T(8,128)(2,1)}, u32[]{:S(2)}, u32[]{:S(2)}) async-start(bf16[32,1,1536,128]{2,3,1,0:T(8,128)(2,1)} %stack.2), calls=%async_computation.1 | async-start | bytes 25165824 | tf_op jit(solution)/shard_map/all_to_all | solution.py:23
  384.4 30.8 %all-to-all-start.2 = ((f32[16,1,16]{2,1,0:T(1,128)}), f32[16,1,16]{2,1,0:T(1,128)S(1)}, u32[]{:S(2)}, u32[]{:S(2)}) async-start(f32[16,1,16]{2,1,0:T(1,128)} %all_to_all.16), calls=%async_computation.2 | async-start | bytes 16384 | tf_op jit(solution)/shard_map/all_to_all | solution.py:76
